TPU v7x, 512 devices: a whole 4x8x8 slice. The times are simulated.
512 devices in a mesh: vocab: 4 (over x), rows: 128 (over y, z, core).
Axes of the slice: x: 4, y: 8, z: 8, core: 2. Of those that a mesh axis runs over, the one named last changes fastest.
Arguments:
- hidden: bfloat16 [4, 4096, 8192], P(None, 'rows'), may hold values from -0.75 to 0.75
- teacher_weight: bfloat16 [8192, 1536], P('rows', 'vocab'), may hold values from -20 to 20
- draft_weight: bfloat16 [8192, 512], P('rows', 'vocab'), may hold values from -20 to 20
- draft_list: int32 [4, 4], replicated, may hold values from 0 to 11, as said below
Outputs:
- row_loss: float32 [4, 4096], P(None, 'rows')
- grad_hidden: bfloat16 [4, 4096, 8192], P(None, 'rows')
- grad_draft: float32 [8192, 512], P('rows', 'vocab')
Inputs may be any that keep to these rules, and one draw needn't show every extreme that they name: `draft_list`: in each tile the 4 listed blocks are distinct.
All inputs are finite; a program needn't handle non-finite values.
Results may differ from a plain program's by a relative error of at most 0.008.
Values may be sent and summed in bfloat16 or wider, within the bound.
A program may use at most 64 MiB of HBM per device.

v0:
```python
import jax
import jax.numpy as jnp
from jax import lax
from jax.sharding import PartitionSpec as P

BLK = 128


def pick_blocks(tile_blocks, listed):
    return jnp.take(tile_blocks, listed, axis=1)


def per_device(hidden, teacher_weight, draft_weight, draft_list):
    tile_count, tile_rows, model_width = hidden.shape
    row_count = tile_count * tile_rows
    flat_rows = hidden.reshape(row_count, model_width)
    draft_cols = draft_weight.shape[1]
    slot_count = draft_cols // BLK
    columns = flat_rows
    teacher_logits = jnp.dot(
        columns,
        lax.all_gather(teacher_weight, "rows", axis=0, tiled=True),
        preferred_element_type=jnp.float32,
    )
    draft_full = lax.all_gather(draft_weight, "rows", axis=0, tiled=True)
    draft_logits = jnp.dot(flat_rows, draft_full, preferred_element_type=jnp.float32)
    teacher_all = lax.all_gather(teacher_logits, "vocab", axis=1, tiled=True)
    teacher_max = jnp.max(teacher_all, axis=1, keepdims=True)
    teacher_total = jnp.sum(jnp.exp(teacher_all - teacher_max), axis=1, keepdims=True)
    blocks = teacher_all.reshape(tile_count, tile_rows, -1, BLK)
    picked = jax.vmap(pick_blocks)(blocks, draft_list)
    target = jnp.exp(
        picked - teacher_max.reshape(tile_count, tile_rows, 1, 1)
    ) / teacher_total.reshape(tile_count, tile_rows, 1, 1)
    covered = jnp.sum(target, axis=(2, 3)).reshape(row_count)
    vocab_position = lax.axis_index("vocab")
    own_target = lax.dynamic_slice_in_dim(
        target, vocab_position * slot_count, slot_count, 2
    ).reshape(row_count, draft_cols)
    local_max = jnp.max(draft_logits, axis=1)
    weighted = jnp.sum(own_target * draft_logits, axis=1)
    draft_max = lax.pmax(local_max, "vocab")
    local_total = jnp.sum(jnp.exp(draft_logits - draft_max[:, None]), axis=1)
    draft_total, crossed = lax.psum((local_total, weighted), "vocab")
    row_loss = covered * (draft_max + jnp.log(draft_total)) - crossed
    draft_prob = jnp.exp(draft_logits - draft_max[:, None]) / draft_total[:, None]
    logit_grad = (covered[:, None] * draft_prob - own_target).astype(jnp.bfloat16)
    partial_value = lax.dot_general(
        logit_grad, draft_full, (((1,), (1,)), ((), ())), preferred_element_type=jnp.float32
    )
    grad_hidden = lax.psum(partial_value.astype(jnp.bfloat16), "vocab").reshape(
        tile_count, tile_rows, model_width
    )
    columns = flat_rows
    grad_draft = lax.psum_scatter(
        lax.dot_general(
            columns, logit_grad, (((0,), (0,)), ((), ())), preferred_element_type=jnp.float32
        ),
        "rows",
        scatter_dimension=0,
        tiled=True,
    )
    return (row_loss.reshape(tile_count, tile_rows), grad_hidden, grad_draft)


def solution(mesh):
    in_specs = (P(None, "rows", None), P("rows", "vocab"), P("rows", "vocab"), P())
    out_specs = (P(None, "rows"), P(None, "rows", None), P("rows", "vocab"))
    return jax.shard_map(
        per_device, mesh=mesh, in_specs=in_specs, out_specs=out_specs, check_vma=False
    )
```

profile of v0, /device:TPU:2, one launch (start us, length us, event | category | flops | bytes accessed | tf_op | source)
XLA Modules:
  0.0 502.0 jit_solution(2816774992845677760)
XLA Ops:
  7.2 0.0 copy-start
  7.2 0.0 all-gather.5.cloned.1.call-start
  7.2 0.7 all-gather.5.cloned.1.call-update
  7.9 0.0 all-gather.3.cloned.1.call-start
  8.0 0.7 all-gather.3.cloned.1.call-update
  8.7 0.0 all-reduce.3.cloned.1.call-start
  8.7 0.7 compare_and_fusion
  9.4 0.1 copy.16
  9.5 0.7 bitcast_or_fusion
  10.2 0.1 reshape.41
  10.3 88.6 %all-gather.5.cloned.1.call-done = bf16[8192,128]{1,0:T(8,128)(2,1)} async-done(((bf16[64,128]{1,0:T(8,128)(2,1)}), bf16[8192,128]{1,0:T(8,128)(2,1)}) %all-gather.5.cloned.1.call-update) | async-done | bytes 2097168 | tf_op jit(solution)/shard_map/all_gather | solution.py:25
  98.9 0.0 copy-done
  98.9 2.5 fusion.6
  101.4 8.6 %pmax.7 = f32[128]{0:T(128)S(1)} all-reduce(f32[128]{0:T(128)S(1)} %get-tuple-element.18), channel_id=1, replica_groups=mesh['vocab'=4,'rows'=128] {'vocab'}, use_global_device_ids=true, to_apply=%region_4.5 | all-reduce | flops 128 | bytes 1024 | tf_op jit(solution)/shard_map/pmax | solution.py:42
  110.0 74.8 %all-gather.3.cloned.1.call-done = bf16[8192,384]{1,0:T(8,128)(2,1)} async-done(((bf16[64,384]{1,0:T(8,128)(2,1)}), bf16[8192,384]{1,0:T(8,128)(2,1)}) %all-gather.3.cloned.1.call-update) | async-done | bytes 6291472 | tf_op jit(solution)/shard_map/all_gather | solution.py:22
  184.8 4.0 fusion.7
  188.8 14.3 %all_gather.10 = f32[128,1536]{1,0:T(8,128)S(1)} all-gather(f32[128,384]{1,0:T(8,128)S(1)} %fusion.7), channel_id=1, replica_groups=mesh['vocab'=4,'rows'=128] {'vocab'}, dimensions={1}, use_global_device_ids=true | all-gather | bytes 983040 | tf_op jit(solution)/shard_map/all_gather | solution.py:27
  203.1 0.1 reduce_max.18
  203.2 0.3 exponential_reduce_fusion
  203.5 0.1 sub.36
  203.6 1.1 reshape.36
  204.7 0.1 div.18
  204.8 1.5 copy.17
  206.3 0.6 gather_fusion
  206.9 0.2 fusion.4
  207.1 0.1 reshape.37
  207.2 0.1 copy.19
  207.3 7.9 %all-reduce = (f32[128]{0:T(128)S(1)}, f32[128]{0:T(128)S(1)}) all-reduce(f32[128]{0:T(128)S(1)} %get-tuple-element.13, f32[128]{0:T(128)S(1)} %get-tuple-element.12), channel_id=1, replica_groups=mesh['vocab'=4,'rows'=128] {'vocab'}, use_global_device_ids=true, to_apply=%region_8.9 | all-reduce | flops 256 | bytes 2048 | tf_op jit(solution)/shard_map/psum | solution.py:44
  215.3 3.6 convolution_convert_fusion
  218.9 0.0 all-reduce.3.cloned.1.call-update
  219.0 0.0 reduce-scatter.4.cloned.1.call-start
  219.0 2.6 convolution_bitcast_fusion
  221.6 5.6 %copy.22 = f32[8192,128]{1,0:T(8,128)} copy(f32[8192,128]{0,1:T(8,128)} %convolution_bitcast_fusion) | data formatting | bytes 8388608
  227.2 0.0 reduce-scatter.4.cloned.1.call-update
  227.3 0.7 reshape.39
  227.9 56.6 %all-reduce.3.cloned.1.call-done = bf16[4,32,8192]{2,1,0:T(8,128)(2,1)} async-done(((bf16[4,32,8192]{2,1,0:T(8,128)(2,1)}), bf16[4,32,8192]{2,1,0:T(8,128)(2,1)}) %all-reduce.3.cloned.1.call-update) | async-done | bytes 2097168 | tf_op jit(solution)/shard_map/psum | solution.py:51
  284.5 207.9 %reduce-scatter.4.cloned.1.call-done = f32[64,128]{1,0:T(8,128)} async-done(((f32[8192,128]{1,0:T(8,128)}), f32[64,128]{1,0:T(8,128)}) %reduce-scatter.4.cloned.1.call-update) | async-done | bytes 32784
  492.4 3.1 copy.33
  (4 shorter events, 0.1 us)
Async XLA Ops:
  7.2 91.7 %copy-start = (bf16[4,32,8192]{2,1,0:T(8,128)(2,1)S(1)}, bf16[4,32,8192]{2,1,0:T(8,128)(2,1)}, u32[]{:S(2)}) copy-start(bf16[4,32,8192]{2,1,0:T(8,128)(2,1)} %param.4) | copy-start | bytes 6291460
  7.2 91.7 %all-gather.5.cloned.1.call-start = ((), (), s32[]{:S(2)}) async-start(), calls=%async_computation.2 | async-start | bytes 2113536 | tf_op jit(solution)/shard_map/all_gather | solution.py:25
  7.9 176.9 %all-gather.3.cloned.1.call-start = ((), (), s32[]{:S(2)}) async-start(), calls=%async_computation.1 | async-start | bytes 6340608 | tf_op jit(solution)/shard_map/all_gather | solution.py:22
  8.7 275.8 %all-reduce.3.cloned.1.call-start = ((), (), s32[]{:S(2)}) async-start(), calls=%async_computation.3 | async-start | bytes 4194304 | tf_op jit(solution)/shard_map/psum | solution.py:51
  219.0 273.4 %reduce-scatter.4.cloned.1.call-start = ((), (), s32[]{:S(2)}) async-start(), calls=%async_computation.4 | async-start | bytes 4227072
Sparse Core Ops, SparseCore 0:
  11.1 87.7 all-gather.4
  102.0 82.7 all-gather.2
  219.1 65.3 all-reduce.2
  289.3 203.0 reduce-scatter.3
where the time goes:
time: 502 us
  waiting for transfers between devices  429 us (85%)
  blocking collectives  30.8 us (6%)
  between operations  13.8 us (3%)
  local copies, waits for them, and re-layouts  13.1 us (3%)
  matrix products  12.8 us (3%)
    unnamed x5, waiting for transfers between devices  209 us
    all_gather x1, waiting for transfers between devices, per_device(): draft_full = lax.all_gather(draft_weight, 'rows', axis=0, tiled=True)  88.6 us
    all_gather x1, waiting for transfers between devices, per_device(): lax.all_gather(teacher_weight, 'rows', axis=0, tiled=True)  74.8 us
    psum x1, waiting for transfers between devices, per_device(): lax.psum(partial_value.astype(jnp.bfloat16), 'vocab')  56.6 us
    all_gather x1, blocking collectives, per_device(): teacher_all = lax.all_gather(teacher_logits, 'vocab', axis=1, tiled=True)  14.3 us
  transfers between devices with their start and end apart: 4, of which 4 were waited for; matrix products, arithmetic and copies ran while one was open for 3% of the time, Pallas kernels for 0%

commit v1 on v0

--- a/solution.py
+++ b/solution.py
@@ -22,7 +22,9 @@
         lax.all_gather(teacher_weight, "rows", axis=0, tiled=True),
         preferred_element_type=jnp.float32,
     )
-    draft_full = lax.all_gather(draft_weight, "rows", axis=0, tiled=True)
+    draft_full = jnp.concatenate(
+        lax.all_to_all(jnp.stack([draft_weight] * lax.axis_size("rows")), "rows", 0, 0), axis=0
+    )
     draft_logits = jnp.dot(flat_rows, draft_full, preferred_element_type=jnp.float32)
     teacher_all = lax.all_gather(teacher_logits, "vocab", axis=1, tiled=True)
     teacher_max = jnp.max(teacher_all, axis=1, keepdims=True)

time: 502 us -> 452 us (0.900)
  waiting for transfers between devices: 429 us -> 359 us
  starting transfers between devices: 0.16 us -> 18.6 us
    all_gather x1 -> x0, waiting for transfers between devices: 88.6 us -> none  [per_device(): draft_full = lax.all_gather(draft_weight, 'rows', axis=0, tiled=True)]
    all_to_all x0 -> x1, waiting for transfers between devices: none -> 53.6 us  [per_device(): lax.all_to_all(jnp.stack([draft_weight] * lax.axis_size('rows')), 'rows',...]
    all_gather x1, waiting for transfers between devices: 74.8 us -> 39.7 us  [per_device(): lax.all_gather(teacher_weight, 'rows', axis=0, tiled=True)]
    all_to_all x0 -> x1, starting transfers between devices: none -> 18.5 us  [per_device(): lax.all_to_all(jnp.stack([draft_weight] * lax.axis_size('rows')), 'rows',...]
    unnamed x5 -> x4, waiting for transfers between devices: 209 us -> 209 us
where the time goes in v1:
time: 452 us; the launch traced here: 451 us
  waiting for transfers between devices  359 us (79%)
  blocking collectives  30.9 us (7%)
  starting transfers between devices  18.6 us (4%)
  local copies, waits for them, and re-layouts  15.6 us (3%)
  between operations  13.8 us (3%)
  matrix products  12.8 us (3%)
    unnamed x4, waiting for transfers between devices  209 us
    psum x1, waiting for transfers between devices, per_device(): lax.psum(partial_value.astype(jnp.bfloat16), 'vocab')  56.6 us
    all_to_all x1, waiting for transfers between devices, per_device(): lax.all_to_all(jnp.stack([draft_weight] * lax.axis_size('rows')), 'rows',...  53.6 us
    all_gather x1, waiting for transfers between devices, per_device(): lax.all_gather(teacher_weight, 'rows', axis=0, tiled=True)  39.7 us
    all_to_all x1, starting transfers between devices, per_device(): lax.all_to_all(jnp.stack([draft_weight] * lax.axis_size('rows')), 'rows',...  18.5 us
    all_gather x1, blocking collectives, per_device(): teacher_all = lax.all_gather(teacher_logits, 'vocab', axis=1, tiled=True)  14.3 us
  transfers between devices with their start and end apart: 4, of which 4 were waited for; matrix products, arithmetic and copies ran while one was open for 3% of the time, Pallas kernels for 0%

profile of v1, /device:TPU:2, one launch (start us, length us, event | category | flops | bytes accessed | tf_op | source)
XLA Modules:
  0.0 451.3 jit_solution(4469899843100717897)
XLA Ops:
  7.2 0.0 copy-start
  7.2 0.0 all-gather.2.cloned.1.call-start
  7.2 0.7 all-gather.2.cloned.1.call-update
  7.9 2.6 stack.2
  10.5 0.0 copy-start.1
  10.5 18.5 %all-to-all-start = ((bf16[128,64,128]{2,1,0:T(8,128)(2,1)}), bf16[128,64,128]{2,1,0:T(8,128)(2,1)}, u32[]{:S(2)}, u32[]{:S(2)}) async-start(bf16[128,64,128]{2,1,0:T(8,128)(2,1)} %stack.2), calls=%async_computation | async-start | bytes 4194304 | tf_op jit(solution)/shard_map/all_to_all | solution.py:26
  29.0 0.0 all-reduce.3.cloned.1.call-start
  29.0 0.0 copy-done.1
  29.0 0.1 copy.16
  29.1 0.1 reshape.47
  29.2 53.6 %all-to-all-done = bf16[128,64,128]{2,1,0:T(8,128)(2,1)} async-done(((bf16[128,64,128]{2,1,0:T(8,128)(2,1)}), bf16[128,64,128]{2,1,0:T(8,128)(2,1)}, u32[]{:S(2)}, u32[]{:S(2)}) %all-to-all-start) | async-done | bytes 2097184 | tf_op jit(solution)/shard_map/all_to_all | solution.py:26
  82.9 0.0 copy-done
  82.9 2.5 fusion.6
  85.4 8.7 %pmax.7 = f32[128]{0:T(128)S(1)} all-reduce(f32[128]{0:T(128)S(1)} %get-tuple-element.18), channel_id=1, replica_groups=mesh['vocab'=4,'rows'=128] {'vocab'}, use_global_device_ids=true, to_apply=%region_4.5 | all-reduce | flops 128 | bytes 1024 | tf_op jit(solution)/shard_map/pmax | solution.py:44
  94.1 39.7 %all-gather.2.cloned.1.call-done = bf16[8192,384]{1,0:T(8,128)(2,1)} async-done(((bf16[64,384]{1,0:T(8,128)(2,1)}), bf16[8192,384]{1,0:T(8,128)(2,1)}) %all-gather.2.cloned.1.call-update) | async-done | bytes 6291472 | tf_op jit(solution)/shard_map/all_gather | solution.py:22
  133.8 4.0 fusion.7
  137.9 14.3 %all_gather.7 = f32[128,1536]{1,0:T(8,128)S(1)} all-gather(f32[128,384]{1,0:T(8,128)S(1)} %fusion.7), channel_id=1, replica_groups=mesh['vocab'=4,'rows'=128] {'vocab'}, dimensions={1}, use_global_device_ids=true | all-gather | bytes 983040 | tf_op jit(solution)/shard_map/all_gather | solution.py:29
  152.1 0.1 reduce_max.18
  152.3 0.3 exponential_reduce_fusion
  152.5 0.1 sub.36
  152.6 1.1 reshape.41
  153.7 0.1 div.18
  153.8 1.5 copy.17
  155.3 0.6 gather_fusion
  155.9 0.2 fusion.4
  156.1 0.1 reshape.42
  156.2 0.1 copy.19
  156.4 7.9 %all-reduce = (f32[128]{0:T(128)S(1)}, f32[128]{0:T(128)S(1)}) all-reduce(f32[128]{0:T(128)S(1)} %get-tuple-element.13, f32[128]{0:T(128)S(1)} %get-tuple-element.12), channel_id=1, replica_groups=mesh['vocab'=4,'rows'=128] {'vocab'}, use_global_device_ids=true, to_apply=%region_8.9 | all-reduce | flops 256 | bytes 2048 | tf_op jit(solution)/shard_map/psum | solution.py:46
  164.3 3.6 convolution_convert_fusion
  168.0 0.0 all-reduce.3.cloned.1.call-update
  168.0 0.0 reduce-scatter.4.cloned.1.call-start
  168.0 2.6 convolution_bitcast_fusion
  170.7 5.6 %copy.22 = f32[8192,128]{1,0:T(8,128)} copy(f32[8192,128]{0,1:T(8,128)} %convolution_bitcast_fusion) | data formatting | bytes 8388608
  176.2 0.0 reduce-scatter.4.cloned.1.call-update
  176.3 0.7 reshape.45
  176.9 56.6 %all-reduce.3.cloned.1.call-done = bf16[4,32,8192]{2,1,0:T(8,128)(2,1)} async-done(((bf16[4,32,8192]{2,1,0:T(8,128)(2,1)}), bf16[4,32,8192]{2,1,0:T(8,128)(2,1)}) %all-reduce.3.cloned.1.call-update) | async-done | bytes 2097168 | tf_op jit(solution)/shard_map/psum | solution.py:53
  233.5 208.2 %reduce-scatter.4.cloned.1.call-done = f32[64,128]{1,0:T(8,128)} async-done(((f32[8192,128]{1,0:T(8,128)}), f32[64,128]{1,0:T(8,128)}) %reduce-scatter.4.cloned.1.call-update) | async-done | bytes 32784
  441.7 3.1 copy.33
  (6 shorter events, 0.1 us)
Async XLA Ops:
  7.2 75.7 %copy-start = (bf16[4,32,8192]{2,1,0:T(8,128)(2,1)S(1)}, bf16[4,32,8192]{2,1,0:T(8,128)(2,1)}, u32[]{:S(2)}) copy-start(bf16[4,32,8192]{2,1,0:T(8,128)(2,1)} %param.4) | copy-start | bytes 6291460
  7.2 126.6 %all-gather.2.cloned.1.call-start = ((), (), s32[]{:S(2)}) async-start(), calls=%async_computation.2 | async-start | bytes 6340608 | tf_op jit(solution)/shard_map/all_gather | solution.py:22
  10.5 18.5 %copy-start.1 = (s32[4,4]{1,0:T(4,128)S(1)}, s32[4,4]{1,0:T(4,128)}, u32[]{:S(2)}) copy-start(s32[4,4]{1,0:T(4,128)} %param.7) | copy-start | bytes 196
  10.5 72.4 %all-to-all-start = ((bf16[128,64,128]{2,1,0:T(8,128)(2,1)}), bf16[128,64,128]{2,1,0:T(8,128)(2,1)}, u32[]{:S(2)}, u32[]{:S(2)}) async-start(bf16[128,64,128]{2,1,0:T(8,128)(2,1)} %stack.2), calls=%async_computation | async-start | bytes 4194304 | tf_op jit(solution)/shard_map/all_to_all | solution.py:26
  29.0 204.6 %all-reduce.3.cloned.1.call-start = ((), (), s32[]{:S(2)}) async-start(), calls=%async_computation.3 | async-start | bytes 4194304 | tf_op jit(solution)/shard_map/psum | solution.py:53
  168.0 273.7 %reduce-scatter.4.cloned.1.call-start = ((), (), s32[]{:S(2)}) async-start(), calls=%async_computation.4 | async-start | bytes 4227072
Sparse Core Ops, SparseCore 0:
  11.1 122.6 all-gather.1
  168.1 65.3 all-reduce.2
  238.5 203.1 reduce-scatter.3

commit v2 on v0

--- a/solution.py
+++ b/solution.py
@@ -48,9 +48,9 @@
     partial_value = lax.dot_general(
         logit_grad, draft_full, (((1,), (1,)), ((), ())), preferred_element_type=jnp.float32
     )
-    grad_hidden = lax.psum(partial_value.astype(jnp.bfloat16), "vocab").reshape(
-        tile_count, tile_rows, model_width
-    )
+    grad_hidden = jnp.sum(
+        lax.all_gather(partial_value.astype(jnp.bfloat16), "vocab"), axis=0
+    ).reshape(tile_count, tile_rows, model_width)
     columns = flat_rows
     grad_draft = lax.psum_scatter(
         lax.dot_general(

time: 502 us -> 520 us (1.036)
  waiting for transfers between devices: 429 us -> 443 us
  other arithmetic: 2.06 us -> 8.91 us
    all_gather x0 -> x1, waiting for transfers between devices: none -> 76.7 us  [per_device(): lax.all_gather(partial_value.astype(jnp.bfloat16), 'vocab')]
    psum x1 -> x0, waiting for transfers between devices: 56.6 us -> none  [per_device(): lax.psum(partial_value.astype(jnp.bfloat16), 'vocab')]
    reduce_sum x0 -> x1, other arithmetic: none -> 6.85 us  [per_device(): jnp.sum(lax.all_gather(partial_value.astype(jnp.bfloat16), 'vocab'), axis=0)]
    unnamed x5, waiting for transfers between devices: 209 us -> 203 us
  transfers between devices with their start and end apart: 4 -> 4, of which waited for: 4 -> 4; matrix products, arithmetic and copies ran while one was open for 3% -> 4% of each run, Pallas kernels for 0% -> 0%
where the time goes in v2:
time: 520 us; the launch traced here: 519 us
  waiting for transfers between devices  443 us (85%)
  blocking collectives  30.8 us (6%)
  between operations  13.8 us (3%)
  matrix products  12.9 us (2%)
  local copies, waits for them, and re-layouts  9.96 us (2%)
  other arithmetic  8.91 us (2%)
    unnamed x5, waiting for transfers between devices  203 us
    all_gather x1, waiting for transfers between devices, per_device(): draft_full = lax.all_gather(draft_weight, 'rows', axis=0, tiled=True)  88.6 us
    all_gather x1, waiting for transfers between devices, per_device(): lax.all_gather(partial_value.astype(jnp.bfloat16), 'vocab')  76.7 us
    all_gather x1, waiting for transfers between devices, per_device(): lax.all_gather(teacher_weight, 'rows', axis=0, tiled=True)  74.8 us
    all_gather x1, blocking collectives, per_device(): teacher_all = lax.all_gather(teacher_logits, 'vocab', axis=1, tiled=True)  14.3 us
  transfers between devices with their start and end apart: 4, of which 4 were waited for; matrix products, arithmetic and copies ran while one was open for 4% of the time, Pallas kernels for 0%

profile of v2, /device:TPU:2, one launch (start us, length us, event | category | flops | bytes accessed | tf_op | source)
XLA Modules:
  0.0 519.2 jit_solution(13364206522672542824)
XLA Ops:
  7.2 0.0 copy-start
  7.2 0.0 all-gather.7.cloned.1.call-start
  7.2 0.7 all-gather.7.cloned.1.call-update
  7.9 0.0 all-gather.5.cloned.1.call-start
  8.0 0.7 all-gather.5.cloned.1.call-update
  8.7 0.0 all-gather.9.cloned.1.call-start
  8.7 0.7 compare_and_fusion
  9.4 0.1 copy.16
  9.5 0.7 bitcast_or_fusion
  10.2 0.1 reshape.41
  10.3 88.6 %all-gather.7.cloned.1.call-done = bf16[8192,128]{1,0:T(8,128)(2,1)} async-done(((bf16[64,128]{1,0:T(8,128)(2,1)}), bf16[8192,128]{1,0:T(8,128)(2,1)}) %all-gather.7.cloned.1.call-update) | async-done | bytes 2097168 | tf_op jit(solution)/shard_map/all_gather | solution.py:25
  98.9 0.0 copy-done
  98.9 2.5 fusion.6
  101.4 8.6 %pmax.7 = f32[128]{0:T(128)S(1)} all-reduce(f32[128]{0:T(128)S(1)} %get-tuple-element.18), channel_id=1, replica_groups=mesh['vocab'=4,'rows'=128] {'vocab'}, use_global_device_ids=true, to_apply=%region_4.5 | all-reduce | flops 128 | bytes 1024 | tf_op jit(solution)/shard_map/pmax | solution.py:42
  110.0 74.8 %all-gather.5.cloned.1.call-done = bf16[8192,384]{1,0:T(8,128)(2,1)} async-done(((bf16[64,384]{1,0:T(8,128)(2,1)}), bf16[8192,384]{1,0:T(8,128)(2,1)}) %all-gather.5.cloned.1.call-update) | async-done | bytes 6291472 | tf_op jit(solution)/shard_map/all_gather | solution.py:22
  184.8 4.0 fusion.7
  188.8 14.3 %all_gather.16 = f32[128,1536]{1,0:T(8,128)S(1)} all-gather(f32[128,384]{1,0:T(8,128)S(1)} %fusion.7), channel_id=1, replica_groups=mesh['vocab'=4,'rows'=128] {'vocab'}, dimensions={1}, use_global_device_ids=true | all-gather | bytes 983040 | tf_op jit(solution)/shard_map/all_gather | solution.py:27
  203.1 0.1 reduce_max.18
  203.2 0.3 exponential_reduce_fusion
  203.5 0.1 sub.36
  203.6 1.1 reshape.36
  204.7 0.1 div.18
  204.8 1.5 copy.17
  206.3 0.6 gather_fusion
  206.9 0.2 fusion.4
  207.1 0.1 reshape.37
  207.2 0.1 copy.19
  207.3 7.9 %all-reduce = (f32[128]{0:T(128)S(1)}, f32[128]{0:T(128)S(1)}) all-reduce(f32[128]{0:T(128)S(1)} %get-tuple-element.13, f32[128]{0:T(128)S(1)} %get-tuple-element.12), channel_id=1, replica_groups=mesh['vocab'=4,'rows'=128] {'vocab'}, use_global_device_ids=true, to_apply=%region_8.9 | all-reduce | flops 256 | bytes 2048 | tf_op jit(solution)/shard_map/psum | solution.py:44
  215.3 3.6 convolution_convert_fusion
  218.9 0.0 all-gather.9.cloned.1.call-update
  219.0 0.0 reduce-scatter.4.cloned.1.call-start
  219.0 2.7 convolution_bitcast_fusion
  221.7 5.6 %copy.22 = f32[8192,128]{1,0:T(8,128)} copy(f32[8192,128]{0,1:T(8,128)} %convolution_bitcast_fusion) | data formatting | bytes 8388608
  227.2 0.0 reduce-scatter.4.cloned.1.call-update
  227.3 0.7 reshape.39
  227.9 76.7 %all-gather.9.cloned.1.call-done = bf16[512,8192]{1,0:T(8,128)(2,1)} async-done(((bf16[128,8192]{1,0:T(8,128)(2,1)}), bf16[512,8192]{1,0:T(8,128)(2,1)}) %all-gather.9.cloned.1.call-update) | async-done | bytes 8388624 | tf_op jit(solution)/shard_map/all_gather | solution.py:52
  304.7 6.8 %reduce_sum.52 = bf16[128,8192]{1,0:T(8,128)(2,1)} reduce(bf16[4,128,8192]{2,1,0:T(8,128)(2,1)} %bitcast.23, bf16[]{:T(256)} %constant.30.clone.1), dimensions={0}, to_apply=%region_9.10 | reduce | flops 3145728 | bytes 10485762 | tf_op jit(solution)/shard_map/reduce_sum | solution.py:51
  311.5 201.2 %reduce-scatter.4.cloned.1.call-done = f32[64,128]{1,0:T(8,128)} async-done(((f32[8192,128]{1,0:T(8,128)}), f32[64,128]{1,0:T(8,128)}) %reduce-scatter.4.cloned.1.call-update) | async-done | bytes 32784
  (4 shorter events, 0.1 us)
Async XLA Ops:
  7.2 91.7 %copy-start = (bf16[4,32,8192]{2,1,0:T(8,128)(2,1)S(1)}, bf16[4,32,8192]{2,1,0:T(8,128)(2,1)}, u32[]{:S(2)}) copy-start(bf16[4,32,8192]{2,1,0:T(8,128)(2,1)} %param.4) | copy-start | bytes 6291460
  7.2 91.7 %all-gather.7.cloned.1.call-start = ((), (), s32[]{:S(2)}) async-start(), calls=%async_computation.2 | async-start | bytes 2113536 | tf_op jit(solution)/shard_map/all_gather | solution.py:25
  7.9 176.9 %all-gather.5.cloned.1.call-start = ((), (), s32[]{:S(2)}) async-start(), calls=%async_computation.1 | async-start | bytes 6340608 | tf_op jit(solution)/shard_map/all_gather | solution.py:22
  8.7 296.0 %all-gather.9.cloned.1.call-start = ((), (), s32[]{:S(2)}) async-start(), calls=%async_computation.3 | async-start | bytes 10485760 | tf_op jit(solution)/shard_map/all_gather | solution.py:52
  219.0 293.7 %reduce-scatter.4.cloned.1.call-start = ((), (), s32[]{:S(2)}) async-start(), calls=%async_computation.4 | async-start | bytes 4227072
Sparse Core Ops, SparseCore 0:
  11.1 87.7 all-gather.6
  102.0 82.7 all-gather.4
  219.1 85.5 all-gather.8
  309.5 203.1 reduce-scatter.3
